TPU v7x, 32 devices: a whole 2x2x4 slice. The times are simulated.
32 devices in a mesh: band: 16 (over z, x, core), lev: 2 (over y).
Axes of the slice: x: 2, y: 2, z: 4, core: 2. Of those that a mesh axis runs over, the one named last changes fastest.
Arguments:
- field_grid: float32 [3, 8, 384, 2, 1536], P(None, 'lev', 'band'), may hold values from -6 to 6
- increment: float32 [3, 8, 384, 2, 1536], P(None, 'lev', 'band'), may hold values from -6 to 6
- points: int32 [384], P('band'), may hold values from 16 to 1536, as said below
- weights: float32 [384], replicated, may hold values from 0.0013020834 to 0.0052083335
- pair_slot: int32 [384], replicated, may hold values from 0 to 383, each once
- legendre: float32 [384, 384, 769], P(('band', 'lev')), may hold values from -6 to 6
- strength: float32 [3, 8], replicated, may hold values from 1 to 16
Outputs:
- stepped: float32 [3, 8, 384, 2, 1536], P(None, 'lev', 'band')
Inputs may be any that keep to these rules, and one draw needn't show every extreme that they name: points[j] lies within 32 of 16 + 1520 * j // 383, kept within 16 to 1536; the last latitude pair has 1536 cells. `pair_slot`: A permutation of 0 to 383; slot s is held by the device of joint band+lev index s // 12, at place s % 12, which holds legendre[s].
All inputs are finite; a program needn't handle non-finite values.
Results may differ from a plain program's by a relative error of at most 0.0003.
Values sent between devices are 32-bit elements; how exact they have to be, the bound alone decides.
A program may use at most 320 MiB of HBM per device.

v0:
```python
import math
import jax
import jax.numpy as jnp
from jax import lax
from jax.sharding import PartitionSpec as P

TWO_PI = 2.0 * math.pi


def dft_tables(counts, length, wavecount):
    inner = 32
    outer = length // inner
    orders = lax.iota(jnp.int32, wavecount)
    coarse = lax.iota(jnp.int32, outer) * inner
    finer = lax.iota(jnp.int32, inner)
    modulus = counts[:, None, None]
    step_angle = (TWO_PI / counts.astype(jnp.float32))[:, None, None]
    coarse_angle = (coarse[None, :, None] * orders[None, None, :] % modulus).astype(
        jnp.float32
    ) * step_angle
    finer_angle = (finer[None, :, None] * orders[None, None, :] % modulus).astype(
        jnp.float32
    ) * step_angle
    coarse_cos = jnp.cos(coarse_angle)[:, :, None, :]
    coarse_sin = jnp.sin(coarse_angle)[:, :, None, :]
    finer_cos = jnp.cos(finer_angle)[:, None, :, :]
    finer_sin = jnp.sin(finer_angle)[:, None, :, :]
    pair_count = counts.shape[0]
    full_cos = (coarse_cos * finer_cos - coarse_sin * finer_sin).reshape(
        pair_count, length, wavecount
    )
    full_sin = (coarse_sin * finer_cos + coarse_cos * finer_sin).reshape(
        pair_count, length, wavecount
    )
    places = lax.iota(jnp.int32, length)
    live = (places[None, :, None] < modulus) & (orders[None, None, :] <= (modulus - 1) // 2)
    cosines = jnp.where(live, full_cos, 0.0)
    sines = jnp.where(live, -full_sin, 0.0)
    return jnp.concatenate([cosines, sines], axis=2)


def body(field_grid, increment, points, weights, pair_slot, legendre, strength):
    band_count = lax.axis_size("band")
    level_groups = lax.axis_size("lev")
    summed = field_grid + increment
    fields = summed.shape[0]
    local_levels = summed.shape[1]
    band_pairs = summed.shape[2]
    length = summed.shape[4]
    wavecount = length // 2
    pair_total = wavecount // 2
    total_levels = local_levels * level_groups
    regrouped = lax.all_to_all(summed, "lev", split_axis=2, concat_axis=1, tiled=True)
    piece_pairs = band_pairs // level_groups
    counts = lax.dynamic_slice_in_dim(points, lax.axis_index("lev") * piece_pairs, piece_pairs)
    tables = dft_tables(counts, length, wavecount)
    row_count = fields * total_levels * 2
    pair_rows = jnp.moveaxis(regrouped, 2, 0).reshape(piece_pairs, row_count, length)
    spectra = jnp.einsum("pqx,pxk->pqk", pair_rows, tables, precision=lax.Precision.HIGHEST)
    spectra = spectra / counts.astype(jnp.float32)[:, None, None]
    piece_width = 2 * row_count
    by_wave = jnp.transpose(spectra.reshape(piece_pairs, row_count, 2, wavecount), (3, 0, 2, 1))
    by_wave = by_wave.reshape(wavecount, piece_pairs, piece_width)
    slot_ranks = lax.iota(jnp.int32, pair_total)
    pair_of_slot = jnp.zeros((pair_total,), jnp.int32).at[pair_slot].set(slot_ranks)
    wave_order = jnp.stack([pair_of_slot, wavecount - 1 - pair_of_slot], axis=1).reshape(wavecount)
    outgoing = jnp.take(by_wave, wave_order, axis=0)
    slot_count = legendre.shape[0]
    arrived = lax.all_to_all(outgoing, ("band", "lev"), split_axis=0, concat_axis=1, tiled=True)
    arrived = arrived.reshape(2 * slot_count, band_count, level_groups, piece_pairs, piece_width)
    row_width = 4 * fields * total_levels
    arrived = arrived.reshape(2 * slot_count, pair_total, row_width)
    lat_count = arrived.shape[1]
    own_slots = lax.axis_index(("band", "lev")) * slot_count + lax.iota(jnp.int32, slot_count)
    lower_wave = jnp.take(pair_of_slot, own_slots)
    columns = lax.iota(jnp.int32, wavecount + 1)
    second_member = columns[None, :] >= (wavecount - lower_wave)[:, None]
    degree = jnp.where(second_member, columns[None, :] - 1, lower_wave[:, None] + columns[None, :])
    wave_of_column = jnp.where(
        second_member, wavecount - 1 - lower_wave[:, None], lower_wave[:, None]
    )
    parity = jnp.where((degree - wave_of_column) % 2 == 0, 1.0, -1.0)
    weighted = arrived.reshape(slot_count, 2, lat_count, row_width) * weights[None, None, :, None]
    analysed = jnp.einsum("sjc,sejr->scer", legendre, weighted, precision=lax.Precision.HIGHEST)
    analysed = analysed.reshape(slot_count, wavecount + 1, 2, 2, fields * total_levels, 2)
    chosen = jnp.where(second_member[:, :, None, None, None], analysed[:, :, 1], analysed[:, :, 0])
    coefficients = chosen[..., 0] + parity[:, :, None, None] * chosen[..., 1]
    degree_real = degree.astype(jnp.float32)
    degree_ratio = degree_real * (degree_real + 1.0) / float((wavecount - 1) * wavecount)
    damping_rate = strength.reshape(fields * total_levels)
    damping = 1.0 / (1.0 + damping_rate[None, None, :] * (degree_ratio * degree_ratio)[:, :, None])
    damped = coefficients * damping[:, :, None, :]
    second_real = jnp.where(second_member, 1.0, 0.0)
    member_mask = jnp.stack([1.0 - second_real, second_real], axis=2)
    hemisphere_sign = jnp.stack([jnp.ones_like(parity), parity], axis=2)
    spread = damped[:, :, None, :, :, None] * member_mask[:, :, :, None, None, None]
    spread = spread * hemisphere_sign[:, :, None, None, None, :]
    spread = spread.reshape(slot_count, wavecount + 1, 2 * row_width)
    returned = jnp.einsum("sjc,scr->sjr", legendre, spread, precision=lax.Precision.HIGHEST)
    leaving = jnp.transpose(returned.reshape(slot_count, lat_count, 2, row_width), (0, 2, 1, 3))
    leaving = leaving.reshape(2 * slot_count, lat_count, row_width)
    leaving = leaving.reshape(2 * slot_count, band_count, level_groups, piece_pairs, piece_width)
    flat_back = leaving.reshape(2 * slot_count, band_count * level_groups, piece_pairs, piece_width)
    home_rows = lax.all_to_all(flat_back, ("band", "lev"), split_axis=1, concat_axis=0, tiled=True)
    home_rows = home_rows.reshape(wavecount, piece_pairs, piece_width)
    positions = (
        jnp.zeros((wavecount,), jnp.int32).at[wave_order].set(lax.iota(jnp.int32, wavecount))
    )
    restored = jnp.take(home_rows, positions, axis=0)
    spectral_rows = jnp.transpose(
        restored.reshape(wavecount, piece_pairs, 2, row_count), (1, 3, 2, 0)
    )
    spectral_rows = spectral_rows.reshape(piece_pairs, row_count, 2 * wavecount)
    doubling = jnp.where(lax.iota(jnp.int32, 2 * wavecount) % wavecount == 0, 1.0, 2.0)
    grid_rows = jnp.einsum(
        "pqk,pxk->pqx",
        spectral_rows * doubling[None, None, :],
        tables,
        precision=lax.Precision.HIGHEST,
    )
    grid_rows = jnp.moveaxis(grid_rows.reshape(piece_pairs, fields, total_levels, 2, length), 0, 2)
    return lax.all_to_all(grid_rows, "lev", split_axis=1, concat_axis=2, tiled=True)


def solution(mesh):
    return jax.shard_map(
        body,
        mesh=mesh,
        in_specs=(
            P(None, "lev", "band", None, None),
            P(None, "lev", "band", None, None),
            P("band"),
            P(),
            P(),
            P(("band", "lev"), None, None),
            P(),
        ),
        out_specs=P(None, "lev", "band", None, None),
        check_vma=False,
    )
```

profile of v0, /device:TPU:0, one launch (start us, length us, event | category | flops | bytes accessed | tf_op | source)
XLA Modules:
  0.0 824.1 jit_solution(12581593312345706289)
XLA Ops:
  0.0 7.1 copy_add_fusion
  12.3 23.5 %fusion.17 = (f32[12,48,768]{2,1,0:T(8,128)S(1)}, f32[12,48,768]{2,1,0:T(8,128)S(1)}) fusion(f32[12]{0:T(128)S(1)} %broadcast_divide_fusion.1, s32[12]{0:T(128)S(1)} %get-tuple-element.26, s32[48,768]{1,0:T(8,128)S(1)} %iota_multiply_fusion, pred[12]{0:T(512)(128)(4,1)S(1)} %broadcast_compare_fusion), kind=kLoop, calls=%fused_computation.43 | loop fusion | flops 3981312 | bytes 3686508 | tf_op jit(solution)/shard_map/cos | solution.py:24
  35.8 16.5 %fusion.24 = (f32[12,32,768]{2,1,0:T(8,128)S(1)}, f32[12,32,768]{2,1,0:T(8,128)}) fusion(f32[12]{0:T(128)S(1)} %broadcast_divide_fusion.1, s32[12]{0:T(128)S(1)} %get-tuple-element.26, s32[32,768]{1,0:T(8,128)S(1)} %iota_multiply_fusion.1, pred[12]{0:T(512)(128)(4,1)S(1)} %broadcast_compare_fusion), kind=kLoop, calls=%fused_computation.51 | loop fusion | flops 2654208 | bytes 2457708 | tf_op jit(solution)/shard_map/cos | solution.py:26
  52.3 37.0 %multiply_subtract_fusion = (f32[12,48,32,768]{3,2,1,0:T(8,128)}, f32[12,48,32,768]{3,2,1,0:T(8,128)}) fusion(f32[12,32,768]{2,1,0:T(8,128)} %get-tuple-element.17, f32[12,48,768]{2,1,0:T(8,128)S(1)} %get-tuple-element.15, f32[12,32,768]{2,1,0:T(8,128)S(1)} %get-tuple-element.16, f32[12,48,768]{2,1,0:T(8,128)S(1)} %get-tuple-element.14), kind=kLoop, calls=%fused_computation.11 | loop fusion | flops 99090432 | bytes 119144448 | tf_op jit(solution)/shard_map/sub | solution.py:29
  89.3 73.0 %and_select_fusion.1 = (f32[12,1536,768]{2,1,0:T(8,128)}, f32[12,1536,768]{2,1,0:T(8,128)}) fusion(f32[12,48,32,768]{3,2,1,0:T(8,128)} %get-tuple-element.10, pred[12,768]{1,0:T(8,128)(4,1)S(1)} %iota_compare_fusion.2, pred[12,1536]{1,0:T(8,128)(4,1)S(1)} %iota_compare_fusion, f32[12,48,32,768]{3,2,1,0:T(8,128)} %get-tuple-element.11), kind=kLoop, calls=%fused_computation.9 | loop fusion | flops 42467328 | bytes 226520064 | tf_op jit(solution)/shard_map/jit(_where)/select_n | solution.py:37
  175.1 74.6 %broadcast_divide_fusion = f32[12,48,1536]{2,1,0:T(8,128)} fusion(f32[12]{0:T(128)S(1)} %copy-done.5, f32[12,48,1536]{2,1,0:T(8,128)S(1)} %reshape.696, f32[12,1536,768]{2,1,0:T(8,128)} %get-tuple-element.19, f32[12,1536,768]{2,1,0:T(8,128)} %get-tuple-element.18), kind=kOutput, calls=%fused_computation.45 | convolution fusion | flops 16336650240 | bytes 120324144 | tf_op jit(solution)/shard_map/pqx,pxk->pqk/dot_general | solution.py:59
  256.2 6.6 gather_fusion.1
  262.8 7.8 broadcast_select_fusion.1
  270.7 7.9 all-to-all-start.1
  280.3 138.3 %all-to-all-done.1 = f32[768,12,96]{2,1,0:T(8,128)} async-done(((f32[768,12,96]{2,1,0:T(8,128)}), f32[768,12,96]{2,1,0:T(8,128)}, u32[]{:S(2)}, u32[]{:S(2)}) %all-to-all-start.1) | async-done | bytes 3538976 | tf_op jit(solution)/shard_map/all_to_all | solution.py:69
  418.6 4.7 copy.49
  425.1 34.2 %fusion.7 = f32[12,769,2,96]{1,3,2,0:T(8,128)} fusion(f32[12,384,769]{1,2,0:T(8,128)} %param.14, f32[12,2,384,96]{3,1,0,2:T(2,128)S(1)} %broadcast_multiply_fusion.1), kind=kOutput, calls=%fused_computation.27 | convolution fusion | flops 8164343808 | bytes 24800256 | tf_op jit(solution)/shard_map/sjc,sejr->scer/dot_general | solution.py:84
  459.3 10.5 %reshape.700 = f32[12,769,2,2,24,2]{1,5,4,3,2,0:T(2,128)} reshape(f32[12,769,2,96]{1,3,2,0:T(8,128)} %fusion.7) | data formatting | bytes 14174208 | tf_op jit(solution)/shard_map/reshape | solution.py:85
  469.8 5.6 fusion.5
  483.8 10.7 %mul.286 = f32[12,769,192]{1,2,0:T(8,128)} reshape(f32[12,769,2,2,24,2]{1,5,4,3,2,0:T(2,128)} %broadcast_multiply_fusion) | data formatting | bytes 14174208 | tf_op jit(solution)/shard_map/mul | solution.py:97
  494.6 19.0 %fusion.48 = f32[12,192,384]{2,1,0:T(8,128)S(1)} fusion(f32[12,769,192]{1,2,0:T(8,128)} %mul.286, f32[12,384,769]{1,2,0:T(8,128)} %param.14), kind=kOutput, calls=%fused_computation.120 | convolution fusion | flops 8164343808 | bytes 24800256 | tf_op jit(solution)/shard_map/sjc,scr->sjr/dot_general | solution.py:99
  513.6 5.5 copy.53
  526.4 102.2 %all-to-all-done.2 = f32[24,32,12,96]{3,0,2,1:T(8,128)} async-done(((f32[24,32,12,96]{3,0,2,1:T(8,128)}), f32[24,32,12,96]{3,0,2,1:T(8,128)}, u32[]{:S(2)}, u32[]{:S(2)}) %all-to-all-start.2) | async-done | bytes 3538976 | tf_op jit(solution)/shard_map/all_to_all | solution.py:104
  631.4 5.4 copy.55
  636.8 6.6 gather_fusion.2
  643.4 8.0 broadcast_select_fusion
  651.4 5.9 copy.56
  659.8 112.1 %fusion = f32[12,48,1536]{2,1,0:T(8,128)} fusion(f32[12,1536,768]{2,1,0:T(8,128)} %get-tuple-element.19, f32[12,1536,768]{2,1,0:T(8,128)} %get-tuple-element.18, f32[12,48,1536]{2,1,0:T(8,128)S(1)} %bitcast.83, f32[1536]{0:T(1024)S(1)} %fusion.37), kind=kOutput, calls=%fused_computation.6 | convolution fusion | flops 16336650240 | bytes 120330240 | tf_op jit(solution)/shard_map/pqk,pxk->pqx/dot_general | solution.py:115
  777.2 42.9 %all_to_all.66 = f32[3,8,12,2,1536]{4,3,0,2,1:T(2,128)S(1)} all-to-all(f32[3,8,12,2,1536]{4,3,0,2,1:T(2,128)S(1)} %bitcast.91), channel_id=1, replica_groups=mesh['band'=16,'lev'=2] {'lev'}, dimensions={1} | all-to-all | bytes 7077888 | tf_op jit(solution)/shard_map/all_to_all | solution.py:122
  (71 shorter events, 57.9 us)
Async XLA Ops:
  7.1 4.4 copy-start.4
  7.1 160.6 %all-to-all-start = ((f32[3,4,24,2,1536]{4,3,1,0,2:T(2,128)}), f32[3,4,24,2,1536]{4,3,1,0,2:T(2,128)S(1)}, u32[]{:S(2)}, u32[]{:S(2)}) async-start(f32[3,4,24,2,1536]{4,3,1,0,2:T(2,128)} %copy_add_fusion), calls=%async_computation | async-start | bytes 7077888 | tf_op jit(solution)/shard_map/all_to_all | solution.py:53
  89.3 73.0 %copy-start.3 = (s32[384]{0:T(512)S(1)}, s32[384]{0:T(512)}, u32[]{:S(2)}) copy-start(s32[384]{0:T(512)} %param.13) | copy-start | bytes 4612
  170.8 4.2 copy-start.5
  270.7 8.6 %copy-start.2 = (f32[3,8]{1,0:T(4,128)S(1)}, f32[3,8]{1,0:T(4,128)}, u32[]{:S(2)}) copy-start(f32[3,8]{1,0:T(4,128)} %param.15) | copy-start | bytes 292
  270.7 147.9 %all-to-all-start.1 = ((f32[768,12,96]{2,1,0:T(8,128)}), f32[768,12,96]{2,1,0:T(8,128)}, u32[]{:S(2)}, u32[]{:S(2)}) async-start(f32[768,12,96]{2,1,0:T(8,128)} %broadcast_select_fusion.1), calls=%async_computation.1 | async-start | bytes 12582912 | tf_op jit(solution)/shard_map/all_to_all | solution.py:69
  418.6 4.8 copy-start.1
  519.0 3.7 copy-start
  519.0 109.6 %all-to-all-start.2 = ((f32[24,32,12,96]{3,0,2,1:T(8,128)}), f32[24,32,12,96]{3,0,2,1:T(8,128)}, u32[]{:S(2)}, u32[]{:S(2)}) async-start(f32[24,32,12,96]{3,0,2,1:T(8,128)} %bitcast.84), calls=%async_computation.2 | async-start | bytes 9437184 | tf_op jit(solution)/shard_map/all_to_all | solution.py:104
where the time goes:
time: 835 us; the launch traced here: 824 us
  waiting for transfers between devices  241 us (29%)
  matrix products  240 us (29%)
  other arithmetic  187 us (22%)
  local copies, waits for them, and re-layouts  97 us (12%)
  blocking collectives  42.9 us (5%)
  starting transfers between devices  16 us (2%)
    all_to_all x1, waiting for transfers between devices, body(): lax.all_to_all(outgoing, ('band', 'lev'), split_axis=0, concat_axis=1, ti...  138 us
    dot_general x1, matrix products, body(): jnp.einsum('pqk,pxk->pqx', spectral_rows * doubling[None, None, :], table...  112 us
    all_to_all x1, waiting for transfers between devices, body(): lax.all_to_all(flat_back, ('band', 'lev'), split_axis=1, concat_axis=0, t...  102 us
    dot_general x1, matrix products, body(): jnp.einsum('pqx,pxk->pqk', pair_rows, tables, precision=lax.Precision.HIG...  74.6 us
    select_n x1, other arithmetic, dft_tables(): cosines = jnp.where(live, full_cos, 0.0)  73 us
    all_to_all x1, blocking collectives, body(): lax.all_to_all(grid_rows, 'lev', split_axis=1, concat_axis=2, tiled=True)  42.9 us
    sub x1, other arithmetic, dft_tables(): coarse_cos * finer_cos - coarse_sin * finer_sin  37 us
    dot_general x1, matrix products, body(): jnp.einsum('sjc,sejr->scer', legendre, weighted, precision=lax.Precision....  34.2 us
  transfers between devices with their start and end apart: 3, of which 2 were waited for; matrix products, arithmetic and copies ran while one was open for 20% of the time, Pallas kernels for 0%

commit v1 on v0

--- a/solution.py
+++ b/solution.py
@@ -66,7 +66,10 @@
     wave_order = jnp.stack([pair_of_slot, wavecount - 1 - pair_of_slot], axis=1).reshape(wavecount)
     outgoing = jnp.take(by_wave, wave_order, axis=0)
     slot_count = legendre.shape[0]
-    arrived = lax.all_to_all(outgoing, ("band", "lev"), split_axis=0, concat_axis=1, tiled=True)
+    count = lax.axis_size(("band", "lev"))
+    pieces = jnp.stack(jnp.split(outgoing, count, axis=0), axis=0)
+    pieces = lax.all_to_all(pieces, ("band", "lev"), split_axis=0, concat_axis=0)
+    arrived = jnp.concatenate(pieces, axis=1)
     arrived = arrived.reshape(2 * slot_count, band_count, level_groups, piece_pairs, piece_width)
     row_width = 4 * fields * total_levels
     arrived = arrived.reshape(2 * slot_count, pair_total, row_width)

time: 835 us -> 807 us (0.966)
  waiting for transfers between devices: 241 us -> 210 us
    all_to_all x1, waiting for transfers between devices: 138 us -> 104 us  [body(): lax.all_to_all(pieces, ('band', 'lev'), split_axis=0, concat_axis=0)]
  transfers between devices with their start and end apart: 3 -> 3, of which waited for: 2 -> 2; matrix products, arithmetic and copies ran while one was open for 20% -> 21% of each run, Pallas kernels for 0% -> 0%
where the time goes in v1:
time: 807 us; the launch traced here: 796 us
  matrix products  240 us (30%)
  waiting for transfers between devices  210 us (26%)
  other arithmetic  188 us (23%)
  local copies, waits for them, and re-layouts  98.5 us (12%)
  blocking collectives  42.9 us (5%)
  starting transfers between devices  15.7 us (2%)
    dot_general x1, matrix products, body(): jnp.einsum('pqk,pxk->pqx', spectral_rows * doubling[None, None, :], table...  112 us
    all_to_all x1, waiting for transfers between devices, body(): lax.all_to_all(flat_back, ('band', 'lev'), split_axis=1, concat_axis=0, t...  106 us
    all_to_all x1, waiting for transfers between devices, body(): lax.all_to_all(pieces, ('band', 'lev'), split_axis=0, concat_axis=0)  104 us
    dot_general x1, matrix products, body(): jnp.einsum('pqx,pxk->pqk', pair_rows, tables, precision=lax.Precision.HIG...  74.6 us
    select_n x1, other arithmetic, dft_tables(): cosines = jnp.where(live, full_cos, 0.0)  72.9 us
    all_to_all x1, blocking collectives, body(): lax.all_to_all(grid_rows, 'lev', split_axis=1, concat_axis=2, tiled=True)  42.9 us
    sub x1, other arithmetic, dft_tables(): coarse_cos * finer_cos - coarse_sin * finer_sin  37 us
    dot_general x1, matrix products, body(): jnp.einsum('sjc,sejr->scer', legendre, weighted, precision=lax.Precision....  34.6 us
  transfers between devices with their start and end apart: 3, of which 2 were waited for; matrix products, arithmetic and copies ran while one was open for 21% of the time, Pallas kernels for 0%

profile of v1, /device:TPU:0, one launch (start us, length us, event | category | flops | bytes accessed | tf_op | source)
XLA Modules:
  0.0 795.7 jit_solution(6864536886623114751)
XLA Ops:
  0.0 7.1 copy_add_fusion
  12.2 23.8 %fusion.17 = (f32[12,48,768]{2,1,0:T(8,128)S(1)}, f32[12,48,768]{2,1,0:T(8,128)S(1)}) fusion(f32[12]{0:T(128)S(1)} %broadcast_divide_fusion.1, s32[12]{0:T(128)S(1)} %get-tuple-element.26, s32[48,768]{1,0:T(8,128)S(1)} %iota_multiply_fusion, pred[12]{0:T(512)(128)(4,1)S(1)} %broadcast_compare_fusion), kind=kLoop, calls=%fused_computation.43 | loop fusion | flops 3981312 | bytes 3686508 | tf_op jit(solution)/shard_map/cos | solution.py:24
  35.9 16.5 %fusion.24 = (f32[12,32,768]{2,1,0:T(8,128)S(1)}, f32[12,32,768]{2,1,0:T(8,128)}) fusion(f32[12]{0:T(128)S(1)} %broadcast_divide_fusion.1, s32[12]{0:T(128)S(1)} %get-tuple-element.26, s32[32,768]{1,0:T(8,128)S(1)} %iota_multiply_fusion.1, pred[12]{0:T(512)(128)(4,1)S(1)} %broadcast_compare_fusion), kind=kLoop, calls=%fused_computation.51 | loop fusion | flops 2654208 | bytes 2457708 | tf_op jit(solution)/shard_map/cos | solution.py:26
  52.5 37.0 %multiply_subtract_fusion = (f32[12,48,32,768]{3,2,1,0:T(8,128)}, f32[12,48,32,768]{3,2,1,0:T(8,128)}) fusion(f32[12,32,768]{2,1,0:T(8,128)} %get-tuple-element.17, f32[12,48,768]{2,1,0:T(8,128)S(1)} %get-tuple-element.15, f32[12,32,768]{2,1,0:T(8,128)S(1)} %get-tuple-element.16, f32[12,48,768]{2,1,0:T(8,128)S(1)} %get-tuple-element.14), kind=kLoop, calls=%fused_computation.11 | loop fusion | flops 99090432 | bytes 119144448 | tf_op jit(solution)/shard_map/sub | solution.py:29
  89.5 72.9 %and_select_fusion.1 = (f32[12,1536,768]{2,1,0:T(8,128)}, f32[12,1536,768]{2,1,0:T(8,128)}) fusion(f32[12,48,32,768]{3,2,1,0:T(8,128)} %get-tuple-element.10, pred[12,768]{1,0:T(8,128)(4,1)S(1)} %iota_compare_fusion.2, pred[12,1536]{1,0:T(8,128)(4,1)S(1)} %iota_compare_fusion, f32[12,48,32,768]{3,2,1,0:T(8,128)} %get-tuple-element.11), kind=kLoop, calls=%fused_computation.9 | loop fusion | flops 42467328 | bytes 226520064 | tf_op jit(solution)/shard_map/jit(_where)/select_n | solution.py:37
  181.3 74.6 %broadcast_divide_fusion = f32[12,48,1536]{2,1,0:T(8,128)} fusion(f32[12]{0:T(128)S(1)} %copy-done.6, f32[12,48,1536]{2,1,0:T(8,128)S(1)} %reshape.698, f32[12,1536,768]{2,1,0:T(8,128)} %get-tuple-element.19, f32[12,1536,768]{2,1,0:T(8,128)} %get-tuple-element.18), kind=kOutput, calls=%fused_computation.45 | convolution fusion | flops 16336650240 | bytes 120324144 | tf_op jit(solution)/shard_map/pqx,pxk->pqk/dot_general | solution.py:59
  262.4 6.7 gather_fusion.1
  269.1 5.0 broadcast_select_fusion.1
  279.0 7.7 all-to-all-start.1
  288.4 103.9 %all-to-all-done.1 = f32[32,24,12,96]{3,1,2,0:T(8,128)} async-done(((f32[32,24,12,96]{3,1,2,0:T(8,128)}), f32[32,24,12,96]{3,1,2,0:T(8,128)}, u32[]{:S(2)}, u32[]{:S(2)}) %all-to-all-start.1) | async-done | bytes 3538976 | tf_op jit(solution)/shard_map/all_to_all | solution.py:71
  396.4 34.6 %fusion.7 = f32[12,769,2,96]{1,3,2,0:T(8,128)} fusion(f32[12,384,769]{1,2,0:T(8,128)} %param.14, f32[12,2,384,96]{3,1,0,2:T(2,128)S(1)} %broadcast_multiply_fusion.1), kind=kOutput, calls=%fused_computation.27 | convolution fusion | flops 8164343808 | bytes 24800256 | tf_op jit(solution)/shard_map/sjc,sejr->scer/dot_general | solution.py:87
  431.0 10.4 %reshape.703 = f32[12,769,2,2,24,2]{1,5,4,3,2,0:T(2,128)} reshape(f32[12,769,2,96]{1,3,2,0:T(8,128)} %fusion.7) | data formatting | bytes 14174208 | tf_op jit(solution)/shard_map/reshape | solution.py:88
  441.5 5.6 fusion.5
  451.0 4.5 broadcast_multiply_fusion
  455.5 10.7 %mul.286 = f32[12,769,192]{1,2,0:T(8,128)} reshape(f32[12,769,2,2,24,2]{1,5,4,3,2,0:T(2,128)} %broadcast_multiply_fusion) | data formatting | bytes 14174208 | tf_op jit(solution)/shard_map/mul | solution.py:100
  466.2 18.6 %fusion.80 = f32[12,192,384]{2,1,0:T(8,128)S(1)} fusion(f32[12,769,192]{1,2,0:T(8,128)} %mul.286, f32[12,384,769]{1,2,0:T(8,128)} %param.14), kind=kOutput, calls=%fused_computation.184 | convolution fusion | flops 8164343808 | bytes 24800256 | tf_op jit(solution)/shard_map/sjc,scr->sjr/dot_general | solution.py:102
  484.8 5.4 copy.82
  494.1 105.8 %all-to-all-done.2 = f32[24,32,12,96]{3,0,2,1:T(8,128)} async-done(((f32[24,32,12,96]{3,0,2,1:T(8,128)}), f32[24,32,12,96]{3,0,2,1:T(8,128)}, u32[]{:S(2)}, u32[]{:S(2)}) %all-to-all-start.2) | async-done | bytes 3538976 | tf_op jit(solution)/shard_map/all_to_all | solution.py:107
  602.6 5.4 copy.84
  608.0 6.7 gather_fusion.2
  614.6 7.8 broadcast_select_fusion
  622.5 5.9 copy.85
  630.9 112.1 %fusion = f32[12,48,1536]{2,1,0:T(8,128)} fusion(f32[12,1536,768]{2,1,0:T(8,128)} %get-tuple-element.19, f32[12,1536,768]{2,1,0:T(8,128)} %get-tuple-element.18, f32[12,48,1536]{2,1,0:T(8,128)S(1)} %bitcast.210, f32[1536]{0:T(1024)S(1)} %fusion.69), kind=kOutput, calls=%fused_computation.6 | convolution fusion | flops 16336650240 | bytes 120330240 | tf_op jit(solution)/shard_map/pqk,pxk->pqx/dot_general | solution.py:118
  748.6 42.9 %all_to_all.56 = f32[3,8,12,2,1536]{4,3,0,2,1:T(2,128)S(1)} all-to-all(f32[3,8,12,2,1536]{4,3,0,2,1:T(2,128)S(1)} %bitcast.217), channel_id=1, replica_groups=mesh['band'=16,'lev'=2] {'lev'}, dimensions={1} | all-to-all | bytes 7077888 | tf_op jit(solution)/shard_map/all_to_all | solution.py:125
  (104 shorter events, 63.1 us)
Async XLA Ops:
  0.0 11.3 %copy-start.5 = (s32[24]{0:T(128)S(1)}, s32[24]{0:T(128)}, u32[]{:S(2)}) copy-start(s32[24]{0:T(128)} %param.11) | copy-start | bytes 292
  7.1 166.8 %all-to-all-start = ((f32[3,4,24,2,1536]{4,3,1,0,2:T(2,128)}), f32[3,4,24,2,1536]{4,3,1,0,2:T(2,128)S(1)}, u32[]{:S(2)}, u32[]{:S(2)}) async-start(f32[3,4,24,2,1536]{4,3,1,0,2:T(2,128)} %copy_add_fusion), calls=%async_computation | async-start | bytes 7077888 | tf_op jit(solution)/shard_map/all_to_all | solution.py:53
  89.5 73.0 %copy-start.4 = (s32[384]{0:T(512)S(1)}, s32[384]{0:T(512)}, u32[]{:S(2)}) copy-start(s32[384]{0:T(512)} %param.13) | copy-start | bytes 4612
  173.9 7.4 copy-start.6
  258.3 4.2 copy-start
  262.4 6.7 copy-start.1
  279.0 8.4 %copy-start.3 = (f32[3,8]{1,0:T(4,128)S(1)}, f32[3,8]{1,0:T(4,128)}, u32[]{:S(2)}) copy-start(f32[3,8]{1,0:T(4,128)} %param.15) | copy-start | bytes 292
  279.0 113.4 %copy-start.2 = (f32[384]{0:T(512)S(1)}, f32[384]{0:T(512)}, u32[]{:S(2)}) copy-start(f32[384]{0:T(512)} %param.12) | copy-start | bytes 4612
  279.0 113.4 %all-to-all-start.1 = ((f32[32,24,12,96]{3,1,2,0:T(8,128)}), f32[32,24,12,96]{3,1,2,0:T(8,128)}, u32[]{:S(2)}, u32[]{:S(2)}) async-start(f32[32,24,12,96]{3,1,2,0:T(8,128)} %copy.78), calls=%async_computation.1 | async-start | bytes 9437184 | tf_op jit(solution)/shard_map/all_to_all | solution.py:71
  490.2 109.6 %all-to-all-start.2 = ((f32[24,32,12,96]{3,0,2,1:T(8,128)}), f32[24,32,12,96]{3,0,2,1:T(8,128)}, u32[]{:S(2)}, u32[]{:S(2)}) async-start(f32[24,32,12,96]{3,0,2,1:T(8,128)} %bitcast.211), calls=%async_computation.2 | async-start | bytes 9437184 | tf_op jit(solution)/shard_map/all_to_all | solution.py:107
